TPU v7x, 32 devices: a whole 2x2x4 slice. The times are simulated.
32 devices in a mesh: expert: 8 (over z, core), hidden: 4 (over y, x).
Axes of the slice: x: 2, y: 2, z: 4, core: 2. Of those that a mesh axis runs over, the one named last changes fastest.
Arguments:
- inputs: bfloat16 [1536, 2880], P('expert', 'hidden'), may hold values from -6 to 6
- out_grad: bfloat16 [1536, 2880], P('expert', 'hidden'), may hold values from -6 to 6
- expert_ids: int32 [1536, 4], P('expert'), may hold values from 0 to 7, all different within a row; in each aligned block of 192 rows (0 to 191, 192 to 383, ...) at most 144 rows name the same one
- route_weight: float32 [1536, 4], P('expert'), may hold values from 0.1 to 1
- w_gate: bfloat16 [8, 2880, 2880], P('expert', 'hidden'), may hold values from -0.109375 to 0.109375
- w_up: bfloat16 [8, 2880, 2880], P('expert', 'hidden'), may hold values from -0.109375 to 0.109375
- w_down: bfloat16 [8, 2880, 2880], P('expert', 'hidden'), may hold values from -0.109375 to 0.109375
Outputs:
- grad_input: bfloat16 [1536, 2880], P('expert', 'hidden')
- grad_route: float32 [1536, 4], P('expert')
- grad_gate: float32 [8, 2880, 2880], P('expert', 'hidden')
- grad_up: float32 [8, 2880, 2880], P('expert', 'hidden')
- grad_down: float32 [8, 2880, 2880], P('expert', 'hidden')
Inputs may be any that keep to these rules, and one draw needn't show every extreme that they name: `expert_ids`: each token names 4 different experts. Among the 192 tokens of one index of the expert axis no expert is named more than 144 times, a bound that some block reaches.
All inputs are finite; a program needn't handle non-finite values.
Results may differ from a plain program's by a relative error of at most 0.018.
Values may be sent and summed in bfloat16 or wider, within the bound.
No kernel may reach another device: no remote copies, remote signals or barrier semaphores. Data moves between devices by JAX's collectives and lax.ppermute only.
A program may use at most 128 MiB of HBM per device.

v0:
```python
import jax
import jax.numpy as jnp
from jax import lax
from jax.sharding import PartitionSpec as P


def slot_tables(expert_ids, experts, capacity):
    count, top = expert_ids.shape
    flat = expert_ids.reshape(-1)
    onehot = (flat[:, None] == jnp.arange(experts, dtype=jnp.int32)[None, :]).astype(jnp.int32)
    position = jnp.cumsum(onehot, axis=0) - 1
    slot = jnp.sum(onehot * position, axis=1)
    dest = flat * capacity + slot
    table = (
        jnp.zeros((experts * capacity,), jnp.int32)
        .at[dest]
        .set(jnp.arange(count * top, dtype=jnp.int32))
    )
    filled = jnp.zeros((experts * capacity,), jnp.int32).at[dest].set(1)
    return (dest, table, filled)


def pack_rows(values, table, filled, top, experts, capacity):
    picked = values[table // top] * filled.astype(values.dtype)[:, None]
    return picked.reshape(experts, capacity, values.shape[1])


def to_local(buffer, n_groups, local_count):
    rest = buffer.shape[2:]
    shaped = buffer.reshape((n_groups, local_count, buffer.shape[1]) + rest)
    return jnp.swapaxes(shaped, 0, 1).reshape((local_count, n_groups * buffer.shape[1]) + rest)


def from_local(buffer, n_groups, capacity):
    local_count = buffer.shape[0]
    rest = buffer.shape[2:]
    shaped = buffer.reshape((local_count, n_groups, capacity) + rest)
    return jnp.swapaxes(shaped, 0, 1).reshape((n_groups * local_count, capacity) + rest)


def per_device(inputs, out_grad, expert_ids, route_weight, w_gate, w_up, w_down):
    n_groups = lax.axis_size("expert")
    local_count = w_gate.shape[0]
    experts = local_count * n_groups
    tok_count, top = expert_ids.shape
    capacity = 3 * top * tok_count // (2 * experts)
    dest, table, filled = slot_tables(expert_ids, experts, capacity)
    send_weight = (route_weight.reshape(-1)[table] * filled.astype(jnp.float32)).reshape(
        experts, capacity
    )
    send_x = pack_rows(inputs, table, filled, top, experts, capacity)
    send_dy = pack_rows(out_grad, table, filled, top, experts, capacity)
    got_x, got_dy, got_weight = (
        lax.all_to_all(send_x, "expert", split_axis=0, concat_axis=0, tiled=True),
        lax.all_to_all(send_dy, "expert", split_axis=0, concat_axis=0, tiled=True),
        lax.all_to_all(
            send_weight.astype(jnp.bfloat16), "expert", split_axis=0, concat_axis=0, tiled=True
        ).astype(send_weight.dtype),
    )
    rows_x, rows_dy = (
        lax.all_gather(got_x, "hidden", axis=2, tiled=True),
        lax.all_gather(got_dy, "hidden", axis=2, tiled=True),
    )
    xs = to_local(rows_x, n_groups, local_count)
    dys = to_local(rows_dy, n_groups, local_count)
    weights = to_local(got_weight, n_groups, local_count)
    gate = jnp.einsum("esd,efd->esf", xs, w_gate, preferred_element_type=jnp.float32)
    up = jnp.einsum("esd,efd->esf", xs, w_up, preferred_element_type=jnp.float32)
    sig = jax.nn.sigmoid(gate)
    act = gate * sig
    hidden = (act * up).astype(jnp.bfloat16)
    back = jnp.einsum("esd,efd->esf", dys, w_down, preferred_element_type=jnp.float32)
    route_part = jnp.sum(hidden.astype(jnp.float32) * back, axis=2)
    grad_hidden = weights[:, :, None] * back
    scaled = (weights[:, :, None] * dys.astype(jnp.float32)).astype(jnp.bfloat16)
    grad_down = jnp.einsum("esf,esd->efd", hidden, scaled, preferred_element_type=jnp.float32)
    d_gate = (grad_hidden * up * sig * (1.0 + gate * (1.0 - sig))).astype(jnp.bfloat16)
    d_up = (grad_hidden * act).astype(jnp.bfloat16)
    grad_gate = jnp.einsum("esf,esd->efd", d_gate, xs, preferred_element_type=jnp.float32)
    grad_up = jnp.einsum("esf,esd->efd", d_up, xs, preferred_element_type=jnp.float32)
    partial_value = jnp.einsum("esf,efd->esd", d_gate, w_gate, preferred_element_type=jnp.float32)
    partial_value = partial_value + jnp.einsum(
        "esf,efd->esd", d_up, w_up, preferred_element_type=jnp.float32
    )
    route_total = lax.psum(route_part, "hidden")
    route_back = from_local(route_total, n_groups, capacity)
    summed = lax.psum_scatter(
        partial_value.astype(jnp.bfloat16), "hidden", scatter_dimension=2, tiled=True
    ).astype(jnp.float32)
    back_rows, back_route = (
        lax.all_to_all(
            from_local(summed, n_groups, capacity).astype(jnp.bfloat16),
            "expert",
            split_axis=0,
            concat_axis=0,
            tiled=True,
        ).astype(jnp.float32),
        lax.all_to_all(
            route_back.astype(jnp.bfloat16), "expert", split_axis=0, concat_axis=0, tiled=True
        ).astype(route_back.dtype),
    )
    per_pair = back_rows.reshape(experts * capacity, back_rows.shape[2])[dest]
    grad_input = jnp.sum(per_pair.reshape(tok_count, top, per_pair.shape[1]), axis=1).astype(
        jnp.bfloat16
    )
    grad_route = back_route.reshape(-1)[dest].reshape(tok_count, top)
    return (grad_input, grad_route, grad_gate, grad_up, grad_down)


def solution(mesh):
    placed = (
        P("expert", "hidden"),
        P("expert", "hidden"),
        P("expert", None),
        P("expert", None),
        P("expert", "hidden", None),
        P("expert", "hidden", None),
        P("expert", "hidden", None),
    )
    return jax.shard_map(
        per_device,
        mesh=mesh,
        in_specs=placed,
        out_specs=(
            P("expert", "hidden"),
            P("expert", None),
            P("expert", "hidden", None),
            P("expert", "hidden", None),
            P("expert", "hidden", None),
        ),
        check_vma=False,
    )
```

profile of v0, /device:TPU:0, one launch (start us, length us, event | category | flops | bytes accessed | tf_op | source)
XLA Modules:
  0.0 514.7 jit_solution(17609842924973014855)
XLA Ops:
  11.5 3.4 scatter_custom_fusion
  15.0 4.6 gather_fusion.1
  19.5 4.8 gather_fusion.2
  24.4 3.4 scatter_custom_fusion.1
  27.9 3.0 broadcast_multiply_fusion.1
  30.8 48.3 %all_to_all.27 = bf16[8,144,720]{2,1,0:T(8,128)(2,1)} all-to-all(bf16[8,144,720]{2,1,0:T(8,128)(2,1)S(1)} %get-tuple-element.32), channel_id=1, replica_groups=mesh['expert'=8,'hidden'=4] {'expert'}, dimensions={0} | all-to-all | bytes 3317760 | tf_op jit(solution)/shard_map/all_to_all | solution.py:54
  79.1 5.1 copy.57
  84.3 45.2 %all_to_all.28 = bf16[8,144,720]{2,1,0:T(8,128)(2,1)} all-to-all(bf16[8,144,720]{2,1,0:T(8,128)(2,1)S(1)} %copy-done.3), channel_id=1, replica_groups=mesh['expert'=8,'hidden'=4] {'expert'}, dimensions={0} | all-to-all | bytes 3317760 | tf_op jit(solution)/shard_map/all_to_all | solution.py:55
  129.4 5.0 copy.55
  134.8 4.6 gather_fusion
  139.4 8.0 %all_to_all.29 = bf16[8,1,144]{2,1,0:T(2,128)(2,1)S(1)} all-to-all(bf16[8,1,144]{2,1,0:T(2,128)(2,1)S(1)} %convert_element_type.129), channel_id=1, replica_groups=mesh['expert'=8,'hidden'=4] {'expert'}, dimensions={0} | all-to-all | bytes 4608 | tf_op jit(solution)/shard_map/all_to_all | solution.py:56
  147.5 51.6 %all-gather.5.cloned.1.call-done = bf16[8,144,2880]{1,0,2:T(8,128)(2,1)} async-done(((bf16[8,144,720]{1,0,2:T(8,128)(2,1)}), bf16[8,144,2880]{1,0,2:T(8,128)(2,1)}) %all-gather.5.cloned.1.call-update) | async-done | bytes 6635536 | tf_op jit(solution)/shard_map/all_gather | solution.py:61
  199.1 16.3 %copy.58 = bf16[8,144,2880]{2,1,0:T(8,128)(2,1)} copy(bf16[8,144,2880]{1,0,2:T(8,128)(2,1)} %all-gather.5.cloned.1.call-done) | data formatting | bytes 13271040 | tf_op jit(solution)/shard_map/all_gather | solution.py:61
  215.4 11.0 %fusion.10 = f32[1152,720]{0,1:T(8,128)} fusion(bf16[1152,2880]{1,0:T(8,128)(2,1)} %bitcast.60, bf16[1,720,2880]{2,1,0:T(8,128)(2,1)} %param.12), kind=kOutput, calls=%fused_computation.21 | convolution fusion | flops 4777574400 | bytes 14100480 | tf_op jit(solution)/shard_map/esd,efd->esf/dot_general | solution.py:68
  226.4 7.6 %fusion.7 = f32[1152,720]{0,1:T(8,128)} fusion(bf16[1152,2880]{1,0:T(8,128)(2,1)S(1)} %bitcast.63, bf16[1,720,2880]{2,1,0:T(8,128)(2,1)S(1)} %bitcast.69), kind=kOutput, calls=%fused_computation.18 | convolution fusion | flops 4777574400 | bytes 14100480 | tf_op jit(solution)/shard_map/esd,efd->esf/dot_general | solution.py:67
  234.0 82.8 %all-gather.3.cloned.1.call-done = bf16[8,144,2880]{1,0,2:T(8,128)(2,1)} async-done(((bf16[8,144,720]{1,0,2:T(8,128)(2,1)}), bf16[8,144,2880]{1,0,2:T(8,128)(2,1)}) %all-gather.3.cloned.1.call-update) | async-done | bytes 6635536 | tf_op jit(solution)/shard_map/all_gather | solution.py:62
  316.9 15.4 %copy.56 = bf16[8,144,2880]{2,1,0:T(8,128)(2,1)} copy(bf16[8,144,2880]{1,0,2:T(8,128)(2,1)} %all-gather.3.cloned.1.call-done) | data formatting | bytes 13271040 | tf_op jit(solution)/shard_map/all_gather | solution.py:62
  332.2 13.6 %multiply_reduce_fusion = (f32[1152]{0:T(1024)S(1)}, bf16[1152,720]{0,1:T(8,128)(2,1)}, bf16[1152,720]{0,1:T(8,128)(2,1)S(1)}, bf16[1152,720]{0,1:T(8,128)(2,1)}) fusion(f32[1152,720]{0,1:T(8,128)} %fusion.10, f32[1152,720]{0,1:T(8,128)} %fusion.7, f32[1152]{0:T(1024)S(1)} %reshape.232, bf16[1152,2880]{1,0:T(8,128)(2,1)} %bitcast.64, ...), kind=kOutput, calls=%fused_computation.25 | convolution fusion | flops 4793332736 | bytes 22404096 | tf_op jit(solution)/shard_map/esd,efd->esf/dot_general | solution.py:72
  345.9 8.8 %fusion.5 = f32[1152,2880]{0,1:T(8,128)} fusion(bf16[1152,720]{0,1:T(8,128)(2,1)S(1)} %get-tuple-element.27, bf16[1,720,2880]{2,1,0:T(8,128)(2,1)S(1)} %bitcast.71), kind=kOutput, calls=%fused_computation.16 | convolution fusion | flops 4777574400 | bytes 19077120 | tf_op jit(solution)/shard_map/esf,efd->esd/dot_general | solution.py:81
  354.6 15.3 %fusion.1 = bf16[1,1152,2880]{1,2,0:T(8,128)(2,1)} fusion(f32[1152,2880]{0,1:T(8,128)} %fusion.5, bf16[1152,720]{0,1:T(8,128)(2,1)} %get-tuple-element.28, bf16[1,720,2880]{2,1,0:T(8,128)(2,1)} %param.12), kind=kOutput, calls=%fused_computation.10 | convolution fusion | flops 4784209920 | bytes 25712640 | tf_op jit(solution)/shard_map/esf,efd->esd/dot_general | solution.py:82
  370.0 16.9 %psum.7 = bf16[1,1152]{1,0:T(2,128)(2,1)S(1)} all-reduce(f32[1,1152]{1,0:T(1,128)S(1)} %reduce_sum.35), channel_id=1, replica_groups=mesh['expert'=8,'hidden'=4] {'hidden'}, use_global_device_ids=true, to_apply=%region_8.9 | all-reduce | flops 1152 | bytes 6912 | tf_op jit(solution)/shard_map/psum | solution.py:85
  387.6 4.6 all-to-all-start.4
  392.2 11.6 %convolution_bitcast_fusion = f32[1,720,2880]{2,1,0:T(8,128)} fusion(bf16[1152,720]{0,1:T(8,128)(2,1)S(1)} %copy-done.7, bf16[1152,2880]{1,0:T(8,128)(2,1)} %bitcast.61), kind=kOutput, calls=%fused_computation.14 | convolution fusion | flops 4777574400 | bytes 16588800 | tf_op jit(solution)/shard_map/esf,esd->efd/dot_general | solution.py:80
  403.8 40.7 %reduce-scatter.7.cloned.1.call-done = bf16[1,1152,720]{1,2,0:T(8,128)(2,1)} async-done(((bf16[1,1152,2880]{1,2,0:T(8,128)(2,1)}), bf16[1,1152,720]{1,2,0:T(8,128)(2,1)}) %reduce-scatter.7.cloned.1.call-update) | async-done | bytes 1658896
  444.6 3.8 copy.59
  448.4 4.6 all-to-all-start.3
  452.9 11.4 %convolution_bitcast_fusion.1 = f32[1,720,2880]{2,1,0:T(8,128)} fusion(bf16[1152,720]{0,1:T(8,128)(2,1)} %copy-done.6, bf16[1152,2880]{1,0:T(8,128)(2,1)} %bitcast.62), kind=kOutput, calls=%fused_computation.15 | convolution fusion | flops 4777574400 | bytes 16588800 | tf_op jit(solution)/shard_map/esf,esd->efd/dot_general | solution.py:79
  464.3 11.2 %fusion.4 = f32[1,720,2880]{2,1,0:T(8,128)} fusion(bf16[1152,720]{0,1:T(8,128)(2,1)S(1)} %copy-done.8, bf16[1152,2880]{1,0:T(8,128)(2,1)} %bitcast.65, f32[1152]{0:T(1024)S(1)} %reshape.232), kind=kOutput, calls=%fused_computation.13 | convolution fusion | flops 4787527680 | bytes 16593408 | tf_op jit(solution)/shard_map/esf,esd->efd/dot_general | solution.py:76
  475.7 4.5 gather_fusion.4
  480.9 14.0 %all-to-all-done.3 = bf16[8,144,720]{2,1,0:T(8,128)(2,1)S(1)} async-done(((bf16[8,144,720]{2,1,0:T(8,128)(2,1)}), bf16[8,144,720]{2,1,0:T(8,128)(2,1)S(1)}, u32[]{:S(2)}, u32[]{:S(2)}) %all-to-all-start.3) | async-done | bytes 1658912 | tf_op jit(solution)/shard_map/all_to_all | solution.py:91
  497.1 6.1 %gather_fusion.3 = f32[768,720]{1,0:T(8,128)} fusion(f32[1152,720]{1,0:T(8,128)} %bitcast_convert_fusion, s32[1024]{0:T(1024)S(1)} %pad_clamp_fusion.2), kind=kCustom, calls=%fused_computation.3 | custom fusion | bytes 4426752 | tf_op jit(solution)/shard_map/gather | solution.py:102
  503.2 2.6 reshape.230
  (71 shorter events, 11.1 us)
Async XLA Ops:
  7.2 7.8 %copy-start = (bf16[192,720]{1,0:T(8,128)(2,1)S(1)}, bf16[192,720]{1,0:T(8,128)(2,1)}, u32[]{:S(2)}) copy-start(bf16[192,720]{1,0:T(8,128)(2,1)} %param.8) | copy-start | bytes 829444
  7.2 192.0 %all-gather.5.cloned.1.call-start = ((), (), s32[]{:S(2)}) async-start(), calls=%async_computation.7 | async-start | bytes 14745600 | tf_op jit(solution)/shard_map/all_gather | solution.py:61
  15.0 4.6 copy-start.2
  79.1 5.2 %copy-start.3 = (bf16[8,144,720]{2,1,0:T(8,128)(2,1)S(1)}, bf16[8,144,720]{2,1,0:T(8,128)(2,1)}, u32[]{:S(2)}) copy-start(bf16[8,144,720]{2,1,0:T(8,128)(2,1)} %get-tuple-element.31) | copy-start | bytes 4976644
  84.2 232.6 %all-gather.3.cloned.1.call-start = ((), (), s32[]{:S(2)}) async-start(), calls=%async_computation.6 | async-start | bytes 14745600 | tf_op jit(solution)/shard_map/all_gather | solution.py:62
  129.4 5.1 copy-start.5
  134.5 310.1 %reduce-scatter.7.cloned.1.call-start = ((), (), s32[]{:S(2)}) async-start(), calls=%async_computation.8 | async-start | bytes 8294400
  199.1 27.3 %slice-start = ((s8[4239360]{0:T(1024)(128)(4,1)}), s8[45056]{0:T(1024)(128)(4,1)S(1)}, s32[]{:S(2)}) async-start(s8[4239360]{0:T(1024)(128)(4,1)} %bitcast.68), calls=%async_computation.9 | async-start | bytes 90112
  215.4 11.0 %copy-start.4 = (bf16[8,144,2880]{2,1,0:T(8,128)(2,1)S(1)}, bf16[8,144,2880]{2,1,0:T(8,128)(2,1)}, u32[]{:S(2)}) copy-start(bf16[8,144,2880]{2,1,0:T(8,128)(2,1)} %copy.58) | copy-start | bytes 19906564
  215.4 11.0 %slice-start.1 = ((s8[4239360]{0:T(1024)(128)(4,1)}), s8[4194304]{0:T(1024)(128)(4,1)S(1)}, s32[]{:S(2)}) async-start(s8[4239360]{0:T(1024)(128)(4,1)} %bitcast.68), calls=%async_computation.10 | async-start | bytes 8388608
  316.9 29.0 %slice-start.2 = ((s8[4239360]{0:T(1024)(128)(4,1)}), s8[45056]{0:T(1024)(128)(4,1)S(1)}, s32[]{:S(2)}) async-start(s8[4239360]{0:T(1024)(128)(4,1)} %bitcast.70), calls=%async_computation.11 | async-start | bytes 90112
  332.2 13.6 %slice-start.3 = ((s8[4239360]{0:T(1024)(128)(4,1)}), s8[4194304]{0:T(1024)(128)(4,1)S(1)}, s32[]{:S(2)}) async-start(s8[4239360]{0:T(1024)(128)(4,1)} %bitcast.70), calls=%async_computation.12 | async-start | bytes 8388608
  345.8 8.8 %copy-start.6 = (bf16[1152,720]{0,1:T(8,128)(2,1)}, bf16[1152,720]{0,1:T(8,128)(2,1)S(1)}, u32[]{:S(2)}) copy-start(bf16[1152,720]{0,1:T(8,128)(2,1)S(1)} %get-tuple-element.27) | copy-start | bytes 4976644
  370.0 22.3 %copy-start.7 = (bf16[1152,720]{0,1:T(8,128)(2,1)S(1)}, bf16[1152,720]{0,1:T(8,128)(2,1)}, u32[]{:S(2)}) copy-start(bf16[1152,720]{0,1:T(8,128)(2,1)} %get-tuple-element.28) | copy-start | bytes 4976644
  387.6 60.7 %all-to-all-start.4 = ((bf16[8,1,144]{2,1,0:T(2,128)(2,1)}), bf16[8,1,144]{2,1,0:T(2,128)(2,1)S(1)}, u32[]{:S(2)}, u32[]{:S(2)}) async-start(bf16[8,1,144]{2,1,0:T(2,128)(2,1)} %convert_element_type.130), calls=%async_computation.4 | async-start | bytes 16384 | tf_op jit(solution)/shard_map/all_to_all | solution.py:98
  448.4 46.6 %all-to-all-start.3 = ((bf16[8,144,720]{2,1,0:T(8,128)(2,1)}), bf16[8,144,720]{2,1,0:T(8,128)(2,1)S(1)}, u32[]{:S(2)}, u32[]{:S(2)}) async-start(bf16[8,144,720]{2,1,0:T(8,128)(2,1)} %bitcast.11), calls=%async_computation.3 | async-start | bytes 3538944 | tf_op jit(solution)/shard_map/all_to_all | solution.py:91
  452.9 11.4 %copy-start.8 = (bf16[1152,720]{0,1:T(8,128)(2,1)S(1)}, bf16[1152,720]{0,1:T(8,128)(2,1)}, u32[]{:S(2)}) copy-start(bf16[1152,720]{0,1:T(8,128)(2,1)} %get-tuple-element.26) | copy-start | bytes 4976644
  497.1 11.1 %copy-start.1 = (bf16[192,720]{1,0:T(8,128)(2,1)S(1)}, bf16[192,720]{1,0:T(8,128)(2,1)}, u32[]{:S(2)}) copy-start(bf16[192,720]{1,0:T(8,128)(2,1)} %param.8) | copy-start | bytes 829444
Sparse Core Ops, SparseCore 0:
  84.3 114.7 all-gather.4
  201.0 115.8 all-gather.2
  370.1 74.3 reduce-scatter.6
where the time goes:
time: 516 us; the launch traced here: 515 us
  waiting for transfers between devices  189 us (37%)
  blocking collectives  118 us (23%)
  matrix products  90.5 us (18%)
  local copies, waits for them, and re-layouts  83.2 us (16%)
  between operations  14 us (3%)
  other arithmetic  10.2 us (2%)
  starting transfers between devices  9.32 us (2%)
    all_gather x1, waiting for transfers between devices, per_device(): lax.all_gather(got_dy, 'hidden', axis=2, tiled=True)  82.8 us
    all_gather x1, waiting for transfers between devices, per_device(): lax.all_gather(got_x, 'hidden', axis=2, tiled=True)  51.6 us
    all_to_all x1, blocking collectives, per_device(): lax.all_to_all(send_x, 'expert', split_axis=0, concat_axis=0, tiled=True)  48.3 us
    all_to_all x1, blocking collectives, per_device(): lax.all_to_all(send_dy, 'expert', split_axis=0, concat_axis=0, tiled=True)  45.2 us
    unnamed x4, waiting for transfers between devices  40.8 us
    psum x1, blocking collectives, per_device(): route_total = lax.psum(route_part, 'hidden')  16.9 us
    all_gather x1, local copies, waits for them, and re-layouts, per_device(): lax.all_gather(got_x, 'hidden', axis=2, tiled=True)  16.3 us
    all_gather x1, local copies, waits for them, and re-layouts, per_device(): lax.all_gather(got_dy, 'hidden', axis=2, tiled=True)  15.4 us
  transfers between devices with their start and end apart: 5, of which 4 were waited for; matrix products, arithmetic and copies ran while one was open for 17% of the time, Pallas kernels for 0%

commit v1 on v0

--- a/solution.py
+++ b/solution.py
@@ -59,7 +59,9 @@
     )
     rows_x, rows_dy = (
         lax.all_gather(got_x, "hidden", axis=2, tiled=True),
-        lax.all_gather(got_dy, "hidden", axis=2, tiled=True),
+        jnp.concatenate(
+            lax.all_to_all(jnp.stack([got_dy] * lax.axis_size("hidden")), "hidden", 0, 0), axis=2
+        ),
     )
     xs = to_local(rows_x, n_groups, local_count)
     dys = to_local(rows_dy, n_groups, local_count)

time: 516 us -> 512 us (level)
  waiting for transfers between devices: 189 us -> 178 us
  matrix products: 90.5 us -> 80.3 us
  local copies, waits for them, and re-layouts: 83.2 us -> 89.4 us
  starting transfers between devices: 9.32 us -> 15.2 us
    all_to_all x0 -> x1, waiting for transfers between devices: none -> 124 us  [per_device(): lax.all_to_all(jnp.stack([got_dy] * lax.axis_size('hidden')), 'hidden', 0...]
    all_gather x1 -> x0, waiting for transfers between devices: 82.8 us -> none  [per_device(): lax.all_gather(got_dy, 'hidden', axis=2, tiled=True)]
    all_gather x1, waiting for transfers between devices: 51.6 us -> 0.01 us  [per_device(): lax.all_gather(got_x, 'hidden', axis=2, tiled=True)]
    another operation x1 -> x3, local copies, waits for them, and re-layouts: 0.08 us -> 17.5 us
    all_gather x1 -> x0, local copies, waits for them, and re-layouts: 15.4 us -> none  [per_device(): lax.all_gather(got_dy, 'hidden', axis=2, tiled=True)]
    reshape x0 -> x1, local copies, waits for them, and re-layouts: none -> 11.4 us  [per_device(): jnp.concatenate(lax.all_to_all(jnp.stack([got_dy] * lax.axis_size('hidden...]
    all_to_all x0 -> x1, starting transfers between devices: none -> 5.48 us  [per_device(): lax.all_to_all(jnp.stack([got_dy] * lax.axis_size('hidden')), 'hidden', 0...]
    dot_general x1, matrix products: 13.6 us -> 8.4 us  [per_device(): jnp.einsum('esd,efd->esf', dys, w_down, preferred_element_type=jnp.float32)]
  transfers between devices with their start and end apart: 5 -> 5, of which waited for: 4 -> 3; matrix products, arithmetic and copies ran while one was open for 17% -> 15% of each run, Pallas kernels for 0% -> 0%
where the time goes in v1:
time: 512 us; the launch traced here: 506 us
  waiting for transfers between devices  178 us (35%)
  blocking collectives  117 us (23%)
  local copies, waits for them, and re-layouts  89.4 us (17%)
  matrix products  80.3 us (16%)
  starting transfers between devices  15.2 us (3%)
  between operations  14.7 us (3%)
  other arithmetic  10.2 us (2%)
    all_to_all x1, waiting for transfers between devices, per_device(): lax.all_to_all(jnp.stack([got_dy] * lax.axis_size('hidden')), 'hidden', 0...  124 us
    all_to_all x1, blocking collectives, per_device(): lax.all_to_all(send_x, 'expert', split_axis=0, concat_axis=0, tiled=True)  48.1 us
    all_to_all x1, blocking collectives, per_device(): lax.all_to_all(send_dy, 'expert', split_axis=0, concat_axis=0, tiled=True)  44.4 us
    unnamed x3, waiting for transfers between devices  40.7 us
    psum x1, blocking collectives, per_device(): route_total = lax.psum(route_part, 'hidden')  16.9 us
    all_gather x1, local copies, waits for them, and re-layouts, per_device(): lax.all_gather(got_x, 'hidden', axis=2, tiled=True)  15.8 us
    all_to_all x1, waiting for transfers between devices, per_device(): lax.all_to_all(from_local(summed, n_groups, capacity).astype(jnp.bfloat16...  14 us
    another operation x2, local copies, waits for them, and re-layouts  14 us
  transfers between devices with their start and end apart: 5, of which 3 were waited for; matrix products, arithmetic and copies ran while one was open for 15% of the time, Pallas kernels for 0%

profile of v1, /device:TPU:0, one launch (start us, length us, event | category | flops | bytes accessed | tf_op | source)
XLA Modules:
  0.0 505.7 jit_solution(8519041865845613711)
XLA Ops:
  11.5 3.4 scatter_custom_fusion
  15.0 3.4 scatter_custom_fusion.1
  18.5 4.6 gather_fusion.1
  23.1 4.8 gather_fusion.2
  27.9 3.0 broadcast_multiply_fusion.1
  30.9 48.1 %all_to_all.32 = bf16[8,144,720]{2,1,0:T(8,128)(2,1)S(1)} all-to-all(bf16[8,144,720]{2,1,0:T(8,128)(2,1)S(1)} %get-tuple-element.32), channel_id=1, replica_groups=mesh['expert'=8,'hidden'=4] {'expert'}, dimensions={0} | all-to-all | bytes 3317760 | tf_op jit(solution)/shard_map/all_to_all | solution.py:54
  79.0 3.4 copy.59
  82.7 4.6 gather_fusion
  87.4 8.0 %all_to_all.33 = bf16[8,1,144]{2,1,0:T(2,128)(2,1)S(1)} all-to-all(bf16[8,1,144]{2,1,0:T(2,128)(2,1)S(1)} %convert_element_type.129), channel_id=1, replica_groups=mesh['expert'=8,'hidden'=4] {'expert'}, dimensions={0} | all-to-all | bytes 4608 | tf_op jit(solution)/shard_map/all_to_all | solution.py:56
  95.4 44.4 %all_to_all.34 = bf16[8,144,720]{2,1,0:T(8,128)(2,1)S(1)} all-to-all(bf16[8,144,720]{2,1,0:T(8,128)(2,1)S(1)} %copy-done.3), channel_id=1, replica_groups=mesh['expert'=8,'hidden'=4] {'expert'}, dimensions={0} | all-to-all | bytes 3317760 | tf_op jit(solution)/shard_map/all_to_all | solution.py:55
  139.8 3.5 stack.2
  143.3 5.5 %all-to-all-start.2 = ((bf16[4,8,144,720]{3,2,1,0:T(8,128)(2,1)}), bf16[4,8,144,720]{3,2,1,0:T(8,128)(2,1)}, u32[]{:S(2)}, u32[]{:S(2)}) async-start(bf16[4,8,144,720]{3,2,1,0:T(8,128)(2,1)} %stack.2), calls=%async_computation.2 | async-start | bytes 14155776 | tf_op jit(solution)/shard_map/all_to_all | solution.py:63
  149.4 123.6 %all-to-all-done.2 = bf16[4,8,144,720]{3,2,1,0:T(8,128)(2,1)} async-done(((bf16[4,8,144,720]{3,2,1,0:T(8,128)(2,1)}), bf16[4,8,144,720]{3,2,1,0:T(8,128)(2,1)}, u32[]{:S(2)}, u32[]{:S(2)}) %all-to-all-start.2) | async-done | bytes 6635552 | tf_op jit(solution)/shard_map/all_to_all | solution.py:63
  273.0 11.4 %copy.58 = bf16[8,144,4,720]{3,2,1,0:T(4,128)(2,1)} copy(bf16[8,144,4,720]{3,1,0,2:T(8,128)(2,1)} %bitcast.4) | data formatting | bytes 13271040 | tf_op jit(solution)/shard_map/reshape | solution.py:62
  284.5 13.9 %reshape.229 = bf16[1152,2880]{1,0:T(8,128)(2,1)} reshape(bf16[8,144,4,720]{3,2,1,0:T(4,128)(2,1)} %copy.58) | data formatting | bytes 13271040 | tf_op jit(solution)/shard_map/reshape.5
  298.3 15.8 %copy.60 = bf16[8,144,2880]{2,1,0:T(8,128)(2,1)} copy(bf16[8,144,2880]{1,0,2:T(8,128)(2,1)} %all-gather.2.cloned.1.call-done) | data formatting | bytes 13271040 | tf_op jit(solution)/shard_map/all_gather | solution.py:61
  314.1 9.8 %fusion.10 = f32[1152,720]{0,1:T(8,128)S(1)} fusion(bf16[1152,2880]{1,0:T(8,128)(2,1)} %bitcast.60, bf16[1,720,2880]{2,1,0:T(8,128)(2,1)} %param.12), kind=kOutput, calls=%fused_computation.21 | convolution fusion | flops 4777574400 | bytes 14100480 | tf_op jit(solution)/shard_map/esd,efd->esf/dot_general | solution.py:70
  324.0 5.9 %fusion.7 = f32[1152,720]{0,1:T(8,128)S(1)} fusion(bf16[1152,2880]{1,0:T(8,128)(2,1)S(1)} %bitcast.63, bf16[1,720,2880]{2,1,0:T(8,128)(2,1)S(1)} %bitcast.71), kind=kOutput, calls=%fused_computation.18 | convolution fusion | flops 4777574400 | bytes 14100480 | tf_op jit(solution)/shard_map/esd,efd->esf/dot_general | solution.py:69
  330.0 8.4 %multiply_reduce_fusion = (f32[1152]{0:T(1024)S(1)}, bf16[1152,720]{0,1:T(8,128)(2,1)}, bf16[1152,720]{0,1:T(8,128)(2,1)S(1)}, bf16[1152,720]{0,1:T(8,128)(2,1)S(1)}) fusion(f32[1152,720]{0,1:T(8,128)S(1)} %fusion.10, f32[1152,720]{0,1:T(8,128)S(1)} %fusion.7, f32[1152]{0:T(1024)S(1)} %reshape.238, bf16[1152,2880]{1,0:T(8,128)(2,1)S(1)} %bitcast.65, ...), kind=kOutput, calls=%fused_computation.25 | convolution fusion | flops 4793332736 | bytes 22404096 | tf_op jit(solution)/shard_map/esd,efd->esf/dot_general | solution.py:74
  338.4 8.7 %fusion.5 = f32[1152,2880]{0,1:T(8,128)} fusion(bf16[1152,720]{0,1:T(8,128)(2,1)S(1)} %get-tuple-element.27, bf16[1,720,2880]{2,1,0:T(8,128)(2,1)S(1)} %bitcast.71), kind=kOutput, calls=%fused_computation.16 | convolution fusion | flops 4777574400 | bytes 19077120 | tf_op jit(solution)/shard_map/esf,efd->esd/dot_general | solution.py:83
  347.1 13.3 %fusion.1 = bf16[1,1152,2880]{1,2,0:T(8,128)(2,1)} fusion(f32[1152,2880]{0,1:T(8,128)} %fusion.5, bf16[1152,720]{0,1:T(8,128)(2,1)S(1)} %get-tuple-element.28, bf16[1,720,2880]{2,1,0:T(8,128)(2,1)} %param.12), kind=kOutput, calls=%fused_computation.10 | convolution fusion | flops 4784209920 | bytes 25712640 | tf_op jit(solution)/shard_map/esf,efd->esd/dot_general | solution.py:84
  360.4 16.9 %psum.7 = bf16[1,1152]{1,0:T(2,128)(2,1)S(1)} all-reduce(f32[1,1152]{1,0:T(1,128)S(1)} %reduce_sum.35), channel_id=1, replica_groups=mesh['expert'=8,'hidden'=4] {'hidden'}, use_global_device_ids=true, to_apply=%region_8.9 | all-reduce | flops 1152 | bytes 6912 | tf_op jit(solution)/shard_map/psum | solution.py:87
  378.1 4.6 all-to-all-start.5
  382.6 11.6 %convolution_bitcast_fusion.1 = f32[1,720,2880]{2,1,0:T(8,128)} fusion(bf16[1152,720]{0,1:T(8,128)(2,1)S(1)} %copy-done.8, bf16[1152,2880]{1,0:T(8,128)(2,1)} %bitcast.61), kind=kOutput, calls=%fused_computation.15 | convolution fusion | flops 4777574400 | bytes 16588800 | tf_op jit(solution)/shard_map/esf,esd->efd/dot_general | solution.py:81
  394.2 40.7 %reduce-scatter.7.cloned.1.call-done = bf16[1,1152,720]{1,2,0:T(8,128)(2,1)} async-done(((bf16[1,1152,2880]{1,2,0:T(8,128)(2,1)}), bf16[1,1152,720]{1,2,0:T(8,128)(2,1)}) %reduce-scatter.7.cloned.1.call-update) | async-done | bytes 1658896
  435.0 3.8 copy.61
  438.8 4.6 all-to-all-start.4
  443.4 11.4 %convolution_bitcast_fusion = f32[1,720,2880]{2,1,0:T(8,128)} fusion(bf16[1152,720]{0,1:T(8,128)(2,1)} %copy-done.6, bf16[1152,2880]{1,0:T(8,128)(2,1)} %bitcast.62), kind=kOutput, calls=%fused_computation.14 | convolution fusion | flops 4777574400 | bytes 16588800 | tf_op jit(solution)/shard_map/esf,esd->efd/dot_general | solution.py:82
  454.8 11.2 %fusion.4 = f32[1,720,2880]{2,1,0:T(8,128)} fusion(bf16[1152,720]{0,1:T(8,128)(2,1)S(1)} %copy-done.9, bf16[1152,2880]{1,0:T(8,128)(2,1)} %reshape.229, f32[1152]{0:T(1024)S(1)} %reshape.238), kind=kOutput, calls=%fused_computation.13 | convolution fusion | flops 4787527680 | bytes 16593408 | tf_op jit(solution)/shard_map/esf,esd->efd/dot_general | solution.py:78
  466.1 4.5 gather_fusion.4
  471.4 14.0 %all-to-all-done.4 = bf16[8,144,720]{2,1,0:T(8,128)(2,1)S(1)} async-done(((bf16[8,144,720]{2,1,0:T(8,128)(2,1)}), bf16[8,144,720]{2,1,0:T(8,128)(2,1)S(1)}, u32[]{:S(2)}, u32[]{:S(2)}) %all-to-all-start.4) | async-done | bytes 1658912 | tf_op jit(solution)/shard_map/all_to_all | solution.py:93
  487.5 6.1 %gather_fusion.3 = f32[768,720]{1,0:T(8,128)} fusion(f32[1152,720]{1,0:T(8,128)} %bitcast_convert_fusion, s32[1024]{0:T(1024)S(1)} %pad_clamp_fusion.2), kind=kCustom, calls=%fused_computation.3 | custom fusion | bytes 4426752 | tf_op jit(solution)/shard_map/gather | solution.py:104
  (78 shorter events, 14.1 us)
Async XLA Ops:
  7.2 11.3 %copy-start = (bf16[192,720]{1,0:T(8,128)(2,1)S(1)}, bf16[192,720]{1,0:T(8,128)(2,1)}, u32[]{:S(2)}) copy-start(bf16[192,720]{1,0:T(8,128)(2,1)} %param.8) | copy-start | bytes 829444
  7.2 291.2 %all-gather.2.cloned.1.call-start = ((), (), s32[]{:S(2)}) async-start(), calls=%async_computation.7 | async-start | bytes 14745600 | tf_op jit(solution)/shard_map/all_gather | solution.py:61
  18.5 4.6 copy-start.2
  79.0 3.4 copy-start.5
  82.7 12.7 %copy-start.3 = (bf16[8,144,720]{2,1,0:T(8,128)(2,1)S(1)}, bf16[8,144,720]{2,1,0:T(8,128)(2,1)}, u32[]{:S(2)}) copy-start(bf16[8,144,720]{2,1,0:T(8,128)(2,1)} %get-tuple-element.31) | copy-start | bytes 4976644
  143.3 129.7 %all-to-all-start.2 = ((bf16[4,8,144,720]{3,2,1,0:T(8,128)(2,1)}), bf16[4,8,144,720]{3,2,1,0:T(8,128)(2,1)}, u32[]{:S(2)}, u32[]{:S(2)}) async-start(bf16[4,8,144,720]{3,2,1,0:T(8,128)(2,1)} %stack.2), calls=%async_computation.2 | async-start | bytes 14155776 | tf_op jit(solution)/shard_map/all_to_all | solution.py:63
  148.8 286.2 %reduce-scatter.7.cloned.1.call-start = ((), (), s32[]{:S(2)}) async-start(), calls=%async_computation.8 | async-start | bytes 8294400
  298.3 25.6 %slice-start.4 = ((s8[4239360]{0:T(1024)(128)(4,1)}), s8[45056]{0:T(1024)(128)(4,1)S(1)}, s32[]{:S(2)}) async-start(s8[4239360]{0:T(1024)(128)(4,1)} %bitcast.70), calls=%async_computation.13 | async-start | bytes 90112
  314.1 9.9 %copy-start.4 = (bf16[8,144,2880]{2,1,0:T(8,128)(2,1)S(1)}, bf16[8,144,2880]{2,1,0:T(8,128)(2,1)}, u32[]{:S(2)}) copy-start(bf16[8,144,2880]{2,1,0:T(8,128)(2,1)} %copy.60) | copy-start | bytes 19906564
  314.1 9.9 %slice-start.5 = ((s8[4239360]{0:T(1024)(128)(4,1)}), s8[4194304]{0:T(1024)(128)(4,1)S(1)}, s32[]{:S(2)}) async-start(s8[4239360]{0:T(1024)(128)(4,1)} %bitcast.70), calls=%async_computation.14 | async-start | bytes 8388608
  314.1 15.8 %slice-start = ((s8[6782976]{0:T(1024)(128)(4,1)}), s8[4194304]{0:T(1024)(128)(4,1)S(1)}, s32[]{:S(2)}) async-start(s8[6782976]{0:T(1024)(128)(4,1)} %bitcast.64), calls=%async_computation.9 | async-start | bytes 8388608
  314.1 15.8 %slice-start.2 = ((s8[4239360]{0:T(1024)(128)(4,1)}), s8[4194304]{0:T(1024)(128)(4,1)S(1)}, s32[]{:S(2)}) async-start(s8[4239360]{0:T(1024)(128)(4,1)} %bitcast.68), calls=%async_computation.11 | async-start | bytes 8388608
  324.0 5.9 %slice-start.1 = ((s8[6782976]{0:T(1024)(128)(4,1)}), s8[2588672]{0:T(1024)(128)(4,1)S(1)}, s32[]{:S(2)}) async-start(s8[6782976]{0:T(1024)(128)(4,1)} %bitcast.64), calls=%async_computation.10 | async-start | bytes 5177344
  324.0 5.9 %slice-start.3 = ((s8[4239360]{0:T(1024)(128)(4,1)}), s8[45056]{0:T(1024)(128)(4,1)S(1)}, s32[]{:S(2)}) async-start(s8[4239360]{0:T(1024)(128)(4,1)} %bitcast.68), calls=%async_computation.12 | async-start | bytes 90112
  338.4 8.7 %copy-start.7 = (bf16[1152,720]{0,1:T(8,128)(2,1)}, bf16[1152,720]{0,1:T(8,128)(2,1)S(1)}, u32[]{:S(2)}) copy-start(bf16[1152,720]{0,1:T(8,128)(2,1)S(1)} %get-tuple-element.27) | copy-start | bytes 4976644
  338.4 8.7 %copy-start.6 = (bf16[1152,720]{0,1:T(8,128)(2,1)}, bf16[1152,720]{0,1:T(8,128)(2,1)S(1)}, u32[]{:S(2)}) copy-start(bf16[1152,720]{0,1:T(8,128)(2,1)S(1)} %get-tuple-element.28) | copy-start | bytes 4976644
  360.4 22.3 %copy-start.8 = (bf16[1152,720]{0,1:T(8,128)(2,1)S(1)}, bf16[1152,720]{0,1:T(8,128)(2,1)}, u32[]{:S(2)}) copy-start(bf16[1152,720]{0,1:T(8,128)(2,1)} %copy-done.7) | copy-start | bytes 4976644
  378.1 60.7 %all-to-all-start.5 = ((bf16[8,1,144]{2,1,0:T(2,128)(2,1)}), bf16[8,1,144]{2,1,0:T(2,128)(2,1)S(1)}, u32[]{:S(2)}, u32[]{:S(2)}) async-start(bf16[8,1,144]{2,1,0:T(2,128)(2,1)} %convert_element_type.130), calls=%async_computation.5 | async-start | bytes 16384 | tf_op jit(solution)/shard_map/all_to_all | solution.py:100
  438.8 46.6 %all-to-all-start.4 = ((bf16[8,144,720]{2,1,0:T(8,128)(2,1)}), bf16[8,144,720]{2,1,0:T(8,128)(2,1)S(1)}, u32[]{:S(2)}, u32[]{:S(2)}) async-start(bf16[8,144,720]{2,1,0:T(8,128)(2,1)} %bitcast.11), calls=%async_computation.4 | async-start | bytes 3538944 | tf_op jit(solution)/shard_map/all_to_all | solution.py:93
  443.4 11.4 %copy-start.9 = (bf16[1152,720]{0,1:T(8,128)(2,1)S(1)}, bf16[1152,720]{0,1:T(8,128)(2,1)}, u32[]{:S(2)}) copy-start(bf16[1152,720]{0,1:T(8,128)(2,1)} %get-tuple-element.26) | copy-start | bytes 4976644
  487.5 11.1 %copy-start.1 = (bf16[192,720]{1,0:T(8,128)(2,1)S(1)}, bf16[192,720]{1,0:T(8,128)(2,1)}, u32[]{:S(2)}) copy-start(bf16[192,720]{1,0:T(8,128)(2,1)} %param.8) | copy-start | bytes 829444
Sparse Core Ops, SparseCore 0:
  82.6 190.6 all-gather.1
  360.5 74.3 reduce-scatter.6
